TPU v7x, 128 devices: a whole 4x4x4 slice. The times are simulated.
128 devices in a mesh: row: 8 (over z_hi, x), blk: 16 (over z_lo, y, core).
Axes of the slice: x: 4, y: 4, z: 4 (z_hi: 2, z_lo: 2; z = z_hi * 2 + z_lo), core: 2. Of those that a mesh axis runs over, the one named last changes fastest.
Arguments:
- spike_counts: int32 [16384, 2048], P(('row', 'blk')), may hold values from 0 to 23, as said below
- kernel_taps: int32 [16], replicated, may hold values from 1 to 8
- lag_bins: int32 [2], replicated, may hold values from 1 to 32, as said below
Outputs:
- correlogram: bfloat16 [2, 16384, 8, 2048], P(None, 'row', None, 'blk')
Inputs may be any that keep to these rules, and one draw needn't show every extreme that they name: `spike_counts`: neurons fire at different rates and share a common drive. `lag_bins`: the second lag equals 32; the first lies between 1 and 31.
All inputs are finite; a program needn't handle non-finite values.
Results may differ from a plain program's by a relative error of at most 0.0034.
Values may be sent and summed in bfloat16 or wider, within the bound.
A program may use at most 128 MiB of HBM per device.

v0:
```python
import jax
import jax.numpy as jnp
from jax import lax
from jax.sharding import PartitionSpec as P

NEURONS = 16384
BINS = 2048
TAPS = 16


def smoothed(spike_counts, kernel_taps):
    counts = spike_counts.astype(jnp.float32)
    weights = kernel_taps.astype(jnp.float32) / jnp.sum(kernel_taps.astype(jnp.float32))
    padded = jnp.pad(counts, ((0, 0), (TAPS - 1, 0)))
    result = jnp.zeros_like(counts)
    for delay in range(TAPS):
        result = result + weights[delay] * padded[:, TAPS - 1 - delay : TAPS - 1 - delay + BINS]
    return result


def later_bins(data, lag):
    padded = jnp.pad(data, ((0, 0), (0, BINS)))
    return lax.dynamic_slice_in_dim(padded, lag, BINS, 1)


def shards(spike_counts, kernel_taps, lag_bins):
    smooth = smoothed(spike_counts, kernel_taps)
    centred = smooth - jnp.mean(smooth, axis=1, keepdims=True)
    totals = lax.psum(jnp.sum(centred, axis=0), ("row", "blk"))
    residual_part = centred - (totals / NEURONS)[None, :]
    zscored = (
        residual_part
        * lax.rsqrt(jnp.mean(residual_part * residual_part, axis=1, keepdims=True) + 1e-05)
    ).astype(jnp.bfloat16)
    span_rows = zscored.shape[0]
    groups = lax.axis_size("row")
    columns = lax.all_gather(zscored, "row", axis=0, tiled=True)
    stacked = jnp.concatenate(
        [later_bins(columns, lag_bins[0]), later_bins(columns, lag_bins[1])], axis=0
    )
    piece = lax.all_gather(zscored, "blk", axis=0, tiled=True)
    product = jnp.dot(piece, stacked.T, preferred_element_type=jnp.float32) / BINS
    product = product.reshape(piece.shape[0], 2, groups, span_rows)
    return jnp.transpose(product, (1, 0, 2, 3)).astype(jnp.bfloat16)


def solution(mesh):
    placed = (P(("row", "blk"), None), P(), P())
    return jax.shard_map(
        shards, mesh=mesh, in_specs=placed, out_specs=P(None, "row", None, "blk"), check_vma=False
    )
```

profile of v0, /device:TPU:1, one launch (start us, length us, event | category | flops | bytes accessed | tf_op | source)
XLA Modules:
  0.0 258.9 jit_solution(15566849793997691235)
XLA Ops:
  6.5 0.0 copy-start
  6.5 0.0 all-gather.5.cloned.1.call-start
  6.5 1.3 convert_reduce_fusion
  7.8 1.3 convert_divide_fusion
  9.1 0.7 fusion.8
  9.8 1.3 convert_element_type.25
  11.2 14.1 %fusion.6 = (f32[128]{0:T(128)S(1)}, f32[128,2048]{1,0:T(8,128)S(1)}) fusion(f32[]{:T(128)} %bitcast.15, f32[]{:T(128)} %bitcast.14, f32[]{:T(128)} %bitcast.13, f32[]{:T(128)} %bitcast.12, f32[]{:T(128)} %bitcast.11, f32[]{:T(128)} %bitcast.10, f32[]{:T(128)} %bitcast.9, f32[]{:T(128)} %bitcast.8, f32[]{:T(128)} %bitcast.7, f32[]{:T(128)} %bitcast.6, ...), kind=kLoop, calls=%fused_computation.19 | loop fusion | flops 8388480 | bytes 2097728 | tf_op jit(solution)/shard_map/reduce_sum | solution.py:28
  25.3 0.2 subtract_reduce_fusion
  25.5 68.7 %psum.7 = f32[2048]{0:T(1024)S(1)} all-reduce(f32[2048]{0:T(1024)S(1)} %subtract_reduce_fusion), channel_id=1, replica_groups=mesh['row'=8,'blk'=16] {'row','blk'}, use_global_device_ids=true, to_apply=%region_3.4 | all-reduce | flops 2048 | bytes 16384 | tf_op jit(solution)/shard_map/psum | solution.py:29
  94.2 0.3 multiply_reduce_fusion
  94.5 1.0 multiply_convert_fusion.1
  95.5 0.0 all-gather.5.cloned.1.call-update
  95.6 0.2 all-gather.3.cloned.1.call-start
  95.8 0.5 all-gather.3.cloned.1.call-update
  96.3 0.0 copy-done
  96.3 0.6 fusion.7
  100.7 62.5 %all-gather.5.cloned.1.call-done = bf16[1024,2048]{1,0:T(8,128)(2,1)} async-done(((bf16[128,2048]{1,0:T(8,128)(2,1)}), bf16[1024,2048]{1,0:T(8,128)(2,1)}) %all-gather.5.cloned.1.call-update) | async-done | bytes 4194320 | tf_op jit(solution)/shard_map/all_gather | solution.py:37
  163.2 10.0 %pad_dynamic-slice_fusion.1 = (bf16[1024,2048]{1,0:T(8,128)(2,1)}, bf16[1024,2048]{1,0:T(8,128)(2,1)}) fusion(s32[]{:T(128)S(6)} %select_n.6, bf16[1024,2048]{1,0:T(8,128)(2,1)} %all-gather.5.cloned.1.call-done, s32[]{:T(128)S(6)} %select_n.7), kind=kLoop, calls=%fused_computation.2 | loop fusion | bytes 12582920 | tf_op jit(solution)/shard_map/dynamic_slice | solution.py:23
  173.2 42.5 %all-gather.3.cloned.1.call-done = bf16[2048,2048]{1,0:T(8,128)(2,1)} async-done(((bf16[128,2048]{1,0:T(8,128)(2,1)}), bf16[2048,2048]{1,0:T(8,128)(2,1)}) %all-gather.3.cloned.1.call-update) | async-done | bytes 8388624 | tf_op jit(solution)/shard_map/all_gather | solution.py:41
  215.7 23.8 %multiply_convert_fusion = bf16[2048,2048]{0,1:T(8,128)(2,1)} fusion(bf16[2048,2048]{1,0:T(8,128)(2,1)} %all-gather.3.cloned.1.call-done, bf16[1024,2048]{1,0:T(8,128)(2,1)} %get-tuple-element.8, bf16[1024,2048]{1,0:T(8,128)(2,1)} %get-tuple-element.7), kind=kOutput, calls=%fused_computation | convolution fusion | flops 17205035008 | bytes 25165824 | tf_op jit(solution)/shard_map/dot_general | solution.py:42
  239.5 12.6 %copy.4 = bf16[2048,2,8,128]{3,2,0,1:T(8,128)(2,1)} copy(bf16[2048,2,8,128]{0,3,2,1:T(8,128)(2,1)} %bitcast.21) | data formatting | bytes 16777216 | tf_op jit(solution)/shard_map/convert_element_type | solution.py:44
  (3 shorter events, 0.0 us)
Async XLA Ops:
  6.5 89.8 %copy-start = (s32[2]{0:T(128)S(1)}, s32[2]{0:T(128)}, u32[]{:S(2)}) copy-start(s32[2]{0:T(128)} %param.5) | copy-start | bytes 28
  6.5 156.7 %all-gather.5.cloned.1.call-start = ((), (), s32[]{:S(2)}) async-start(), calls=%async_computation.1 | async-start | bytes 4718592 | tf_op jit(solution)/shard_map/all_gather | solution.py:37
  95.6 120.2 %all-gather.3.cloned.1.call-start = ((), (), s32[]{:S(2)}) async-start(), calls=%async_computation | async-start | bytes 8912896 | tf_op jit(solution)/shard_map/all_gather | solution.py:41
Sparse Core Ops, SparseCore 0:
  95.7 67.5 all-gather.4
  165.0 50.7 all-gather.2
where the time goes:
time: 260 us; the launch traced here: 259 us
  waiting for transfers between devices  106 us (41%)
  blocking collectives  68.7 us (26%)
  local copies, waits for them, and re-layouts  23.9 us (9%)
  matrix products  23.8 us (9%)
  other arithmetic  19.5 us (8%)
  between operations  17.2 us (7%)
    psum x1, blocking collectives, shards(): totals = lax.psum(jnp.sum(centred, axis=0), ('row', 'blk'))  68.7 us
    all_gather x1, waiting for transfers between devices, shards(): columns = lax.all_gather(zscored, 'row', axis=0, tiled=True)  62.5 us
    all_gather x1, waiting for transfers between devices, shards(): piece = lax.all_gather(zscored, 'blk', axis=0, tiled=True)  42.5 us
    dot_general x1, matrix products, shards(): jnp.dot(piece, stacked.T, preferred_element_type=jnp.float32) / BINS  23.8 us
    reduce_sum x1, other arithmetic, shards(): centred = smooth - jnp.mean(smooth, axis=1, keepdims=True)  14.1 us
    convert_element_type x1, local copies, waits for them, and re-layouts, shards(): return jnp.transpose(product, (1, 0, 2, 3)).astype(jnp.bfloat16)  12.6 us
    dynamic_slice x1, local copies, waits for them, and re-layouts, later_bins(): return lax.dynamic_slice_in_dim(padded, lag, BINS, 1)  9.97 us
  transfers between devices with their start and end apart: 2, of which 2 were waited for; matrix products, arithmetic and copies ran while one was open for 4% of the time, Pallas kernels for 0%

commit v1 on v0

--- a/solution.py
+++ b/solution.py
@@ -26,7 +26,7 @@
 def shards(spike_counts, kernel_taps, lag_bins):
     smooth = smoothed(spike_counts, kernel_taps)
     centred = smooth - jnp.mean(smooth, axis=1, keepdims=True)
-    totals = lax.psum(jnp.sum(centred, axis=0), ("row", "blk"))
+    totals = lax.psum(lax.psum(jnp.sum(centred, axis=0), "row"), "blk")
     residual_part = centred - (totals / NEURONS)[None, :]
     zscored = (
         residual_part

time: 260 us -> 242 us (0.931)
  blocking collectives: 68.7 us -> 53.7 us
  waiting for transfers between devices: 106 us -> 103 us
    psum x1 -> x2, blocking collectives: 68.7 us -> 53.7 us  [shards(): totals = lax.psum(lax.psum(jnp.sum(centred, axis=0), 'row'), 'blk')]
where the time goes in v1:
time: 242 us
  waiting for transfers between devices  103 us (43%)
  blocking collectives  53.7 us (22%)
  local copies, waits for them, and re-layouts  23.9 us (10%)
  matrix products  23.8 us (10%)
  other arithmetic  19.5 us (8%)
  between operations  17.2 us (7%)
    all_gather x1, waiting for transfers between devices, shards(): columns = lax.all_gather(zscored, 'row', axis=0, tiled=True)  60.5 us
    psum x2, blocking collectives, shards(): totals = lax.psum(lax.psum(jnp.sum(centred, axis=0), 'row'), 'blk')  53.7 us
    all_gather x1, waiting for transfers between devices, shards(): piece = lax.all_gather(zscored, 'blk', axis=0, tiled=True)  42.5 us
    dot_general x1, matrix products, shards(): jnp.dot(piece, stacked.T, preferred_element_type=jnp.float32) / BINS  23.8 us
    reduce_sum x1, other arithmetic, shards(): centred = smooth - jnp.mean(smooth, axis=1, keepdims=True)  14.1 us
    convert_element_type x1, local copies, waits for them, and re-layouts, shards(): return jnp.transpose(product, (1, 0, 2, 3)).astype(jnp.bfloat16)  12.6 us
    dynamic_slice x1, local copies, waits for them, and re-layouts, later_bins(): return lax.dynamic_slice_in_dim(padded, lag, BINS, 1)  9.97 us
  transfers between devices with their start and end apart: 2, of which 2 were waited for; matrix products, arithmetic and copies ran while one was open for 4% of the time, Pallas kernels for 0%

profile of v1, /device:TPU:1, one launch (start us, length us, event | category | flops | bytes accessed | tf_op | source)
XLA Modules:
  0.0 241.8 jit_solution(10384331034966732726)
XLA Ops:
  6.5 0.0 copy-start
  6.5 0.0 all-gather.5.cloned.1.call-start
  6.5 1.3 convert_reduce_fusion
  7.8 1.3 convert_divide_fusion
  9.1 0.7 fusion.8
  9.8 1.3 convert_element_type.25
  11.2 14.1 %fusion.6 = (f32[128]{0:T(128)S(1)}, f32[128,2048]{1,0:T(8,128)S(1)}) fusion(f32[]{:T(128)} %bitcast.15, f32[]{:T(128)} %bitcast.14, f32[]{:T(128)} %bitcast.13, f32[]{:T(128)} %bitcast.12, f32[]{:T(128)} %bitcast.11, f32[]{:T(128)} %bitcast.10, f32[]{:T(128)} %bitcast.9, f32[]{:T(128)} %bitcast.8, f32[]{:T(128)} %bitcast.7, f32[]{:T(128)} %bitcast.6, ...), kind=kLoop, calls=%fused_computation.19 | loop fusion | flops 8388480 | bytes 2097728 | tf_op jit(solution)/shard_map/reduce_sum | solution.py:28
  25.3 0.2 subtract_reduce_fusion
  25.5 22.4 %psum.14 = f32[2048]{0:T(1024)S(1)} all-reduce(f32[2048]{0:T(1024)S(1)} %subtract_reduce_fusion), channel_id=1, replica_groups=mesh['row'=8,'blk'=16] {'row'}, use_global_device_ids=true, to_apply=%region_3.4 | all-reduce | flops 2048 | bytes 16384 | tf_op jit(solution)/shard_map/psum | solution.py:29
  47.8 31.4 %psum.15 = f32[2048]{0:T(1024)S(1)} all-reduce(f32[2048]{0:T(1024)S(1)} %psum.14), channel_id=1, replica_groups=mesh['row'=8,'blk'=16] {'blk'}, use_global_device_ids=true, to_apply=%region_4.5 | all-reduce | flops 2048 | bytes 16384 | tf_op jit(solution)/shard_map/psum | solution.py:29
  79.2 0.3 multiply_reduce_fusion
  79.5 1.0 multiply_convert_fusion.1
  80.6 0.0 all-gather.5.cloned.1.call-update
  80.6 0.2 all-gather.3.cloned.1.call-start
  80.8 0.5 all-gather.3.cloned.1.call-update
  81.3 0.0 copy-done
  81.4 0.6 fusion.7
  85.8 60.5 %all-gather.5.cloned.1.call-done = bf16[1024,2048]{1,0:T(8,128)(2,1)} async-done(((bf16[128,2048]{1,0:T(8,128)(2,1)}), bf16[1024,2048]{1,0:T(8,128)(2,1)}) %all-gather.5.cloned.1.call-update) | async-done | bytes 4194320 | tf_op jit(solution)/shard_map/all_gather | solution.py:37
  146.2 10.0 %pad_dynamic-slice_fusion.1 = (bf16[1024,2048]{1,0:T(8,128)(2,1)}, bf16[1024,2048]{1,0:T(8,128)(2,1)}) fusion(s32[]{:T(128)S(6)} %select_n.6, bf16[1024,2048]{1,0:T(8,128)(2,1)} %all-gather.5.cloned.1.call-done, s32[]{:T(128)S(6)} %select_n.7), kind=kLoop, calls=%fused_computation.2 | loop fusion | bytes 12582920 | tf_op jit(solution)/shard_map/dynamic_slice | solution.py:23
  156.2 42.5 %all-gather.3.cloned.1.call-done = bf16[2048,2048]{1,0:T(8,128)(2,1)} async-done(((bf16[128,2048]{1,0:T(8,128)(2,1)}), bf16[2048,2048]{1,0:T(8,128)(2,1)}) %all-gather.3.cloned.1.call-update) | async-done | bytes 8388624 | tf_op jit(solution)/shard_map/all_gather | solution.py:41
  198.7 23.8 %multiply_convert_fusion = bf16[2048,2048]{0,1:T(8,128)(2,1)} fusion(bf16[2048,2048]{1,0:T(8,128)(2,1)} %all-gather.3.cloned.1.call-done, bf16[1024,2048]{1,0:T(8,128)(2,1)} %get-tuple-element.8, bf16[1024,2048]{1,0:T(8,128)(2,1)} %get-tuple-element.7), kind=kOutput, calls=%fused_computation | convolution fusion | flops 17205035008 | bytes 25165824 | tf_op jit(solution)/shard_map/dot_general | solution.py:42
  222.4 12.6 %copy.4 = bf16[2048,2,8,128]{3,2,0,1:T(8,128)(2,1)} copy(bf16[2048,2,8,128]{0,3,2,1:T(8,128)(2,1)} %bitcast.21) | data formatting | bytes 16777216 | tf_op jit(solution)/shard_map/convert_element_type | solution.py:44
  (3 shorter events, 0.0 us)
Async XLA Ops:
  6.5 74.8 %copy-start = (s32[2]{0:T(128)S(1)}, s32[2]{0:T(128)}, u32[]{:S(2)}) copy-start(s32[2]{0:T(128)} %param.5) | copy-start | bytes 28
  6.5 139.7 %all-gather.5.cloned.1.call-start = ((), (), s32[]{:S(2)}) async-start(), calls=%async_computation.1 | async-start | bytes 4718592 | tf_op jit(solution)/shard_map/all_gather | solution.py:37
  80.6 118.1 %all-gather.3.cloned.1.call-start = ((), (), s32[]{:S(2)}) async-start(), calls=%async_computation | async-start | bytes 8912896 | tf_op jit(solution)/shard_map/all_gather | solution.py:41
Sparse Core Ops, SparseCore 0:
  80.7 65.4 all-gather.4
  147.9 50.7 all-gather.2
